TPU v7x, 256 devices: a whole 4x4x8 slice. The times are simulated.
256 devices in a mesh: seq: 64 (over z_lo, x, y), tp: 4 (over z_hi, core).
Axes of the slice: x: 4, y: 4, z: 8 (z_hi: 2, z_lo: 4; z = z_hi * 4 + z_lo), core: 2. Of those that a mesh axis runs over, the one named last changes fastest.
Arguments:
- byte_states: bfloat16 [16384, 1024], P('seq'), may hold values from -6 to 6
- enc_gain: bfloat16 [1024], replicated, may hold values from 0.25 to 1.75
- enc_qkv: bfloat16 [3, 1024, 1024], P(None, None, 'tp')
- enc_proj_out: bfloat16 [1024, 1024], P('tp'), may hold values from -0.1875 to 0.1875
- starts: int32 [64, 64], P('seq'), may hold values from 0 to 16384, as said below
- counts: int32 [64], P('seq'), may hold values from 32 to 64, as said below
- lift: bfloat16 [1024, 4096], P(None, 'tp')
- cross_kv: bfloat16 [2, 1024, 4096], P(None, None, 'tp')
- latent_gain: bfloat16 [4096], replicated, may hold values from 0.25 to 1.75
- lat_qkv: bfloat16 [3, 4096, 2048], P(None, 'seq', 'tp')
- lat_proj_out: bfloat16 [2048, 4096], P('tp', 'seq'), may hold values from -0.75 to 0.75
Outputs:
- byte_out: bfloat16 [16384, 1024], P('seq')
- latent_out: bfloat16 [4096, 4096], P('seq', 'tp')
Inputs may be any that keep to these rules, and one draw needn't show every extreme that they name: `starts`: row s lists in increasing order the first byte (counted over all 16384 bytes) of each patch beginning in bytes s * 256 to (s + 1) * 256 - 1, then 16384 in unused places. Byte 0 begins a patch; every row's first patch begins fewer than 8 bytes into its block, and in some row exactly 7 bytes in. counts[s] is the number of patches listed in row s of starts; some row holds 64.
All inputs are finite; a program needn't handle non-finite values.
Results may differ from a plain program's by a relative error of at most 0.018.
Values may be sent and summed in bfloat16 or wider, within the bound.
No kernel may reach another device: no remote copies, remote signals or barrier semaphores. Data moves between devices by JAX's collectives and lax.ppermute only.
A program may use at most 128 MiB of HBM per device.

v0:
```python
import math
import jax
import jax.numpy as jnp
from jax import lax
from jax.sharding import Mesh
from jax.sharding import PartitionSpec as P

EH = 64
HD = 128
WIN = 512
SPILL = 8
SEQ = ("seq_0", "seq_1", "seq_2")
epsilon = 1e-05
rope_base = 500000.0
far_position = 1 << 30


def from_behind(value, axis, steps):
    count = lax.axis_size(axis)
    leading, last = (max(0, -steps), min(count, count - steps))
    return lax.ppermute(value, axis, [(source, source + steps) for source in range(leading, last)])


def from_everyone(value, axis):
    copies = jnp.broadcast_to(value, (lax.axis_size(axis), *value.shape))
    return lax.all_to_all(copies, axis, split_axis=0, concat_axis=0, tiled=True)


def taken_together(value, axis):
    everything = from_everyone(value, axis)
    return jnp.sum(everything, axis=0)


def combined_pairwise(pieces, combine):
    while len(jax.tree.leaves(pieces)[0]) > 1:
        pieces = jax.vmap(combine)(*(pieces[side::2] for side in (0, 1)))
    return pieces[0]


def carried_in(value, axis, combine, identity):
    length, index = (lax.axis_size(axis), lax.axis_index(axis))
    passed = jnp.arange(length) < index

    def kept(part, zero, own):
        part = jnp.where(
            passed.reshape(-1, *(1 for _ in own.shape)), part, jnp.asarray(zero, own.dtype)
        )
        return part

    pieces = from_everyone(value, axis)
    return combined_pairwise(kept(pieces, identity, value), combine)


def laid_out(tiles, dim):
    tiles = jnp.moveaxis(tiles, 0, dim)
    lengths = tiles.shape
    return tiles.reshape(*lengths[:dim], lengths[dim] * lengths[dim + 1], *lengths[dim + 2 :])


def gather_directly(value, axis, dim):
    tiles = from_everyone(value, axis)
    return laid_out(tiles, dim)


def edges_of(length, count):
    unit = 8 if length >= 8 * count else 1
    return [length // unit * k // count * unit for k in range(1, count)]


def gather_in_order(value, axes, turns):
    tiles = value
    for k in turns:
        tiles = lax.all_gather(tiles, axes[k])
    done = turns[::-1]
    back = [done.index(k) for k in range(len(axes))]
    tiles = tiles.transpose(*back, *range(len(axes), tiles.ndim))
    return tiles.reshape(-1, *value.shape)


def spread_gather(value, axes, dim):
    cut = max(range(max(1, value.ndim - 1)), key=lambda d: value.shape[d])
    count, done = (len(axes), [])
    for leading, slab in enumerate(jnp.split(value, edges_of(value.shape[cut], count), axis=cut)):
        if slab.size:
            turns = [(leading - k) % count for k in range(count)]
            done.append(gather_in_order(slab, axes, turns))
    return laid_out(jnp.concatenate(done, axis=cut + 1), dim)


def sent_together(arrays, axis, dim, along):
    ends, at = ([], 0)
    for a in arrays[:-1]:
        at += a.shape[along]
        ends.append(at)
    both = jnp.concatenate(arrays, axis=along)
    return tuple(jnp.split(lax.all_gather(both, axis, axis=dim, tiled=True), ends, axis=along))


def shortened(value):

    def short(part):
        return part.astype(jnp.bfloat16) if part.dtype == jnp.float32 else part

    return jax.tree.map(short, value)


def in_blocks(value, dim, length):
    before, after = (value.shape[:dim], value.shape[dim + 1 :])
    return jnp.moveaxis(value.reshape(*before, length, -1, *after), dim, 0)


def sum_at_owner(value, axis, dim):
    length = lax.axis_size(axis)
    tiles = lax.all_to_all(in_blocks(value, dim, length), axis, 0, 0, tiled=True)
    return jnp.sum(tiles, axis=0)


def rms_scale(values, gain_row):
    mean_square = jnp.mean(values * values, axis=-1, keepdims=True)
    return values * lax.rsqrt(mean_square + epsilon) * gain_row


def masked_softmax(scores, allowed):
    scores = jnp.where(allowed, scores, -1e30)
    largest = jnp.max(scores, axis=-1, keepdims=True)
    raised = jnp.where(allowed, jnp.exp(scores - largest), 0.0)
    return raised / jnp.sum(raised, axis=-1, keepdims=True)


def rotate(values, position):
    halfway = values.shape[-1] // 2
    frequency = jnp.power(
        rope_base, -2.0 * jnp.arange(halfway, dtype=jnp.float32) / values.shape[-1]
    )
    angles = position.astype(jnp.float32)[:, None] * frequency[None, :]
    cosine = jnp.cos(angles)[:, None, :]
    sine_rows = jnp.sin(angles)[:, None, :]
    lower_half = values[..., :halfway]
    upper_half = values[..., halfway:]
    return jnp.concatenate(
        [
            lower_half * cosine - upper_half * sine_rows,
            upper_half * cosine + lower_half * sine_rows,
        ],
        axis=-1,
    )


def patch_block(extended, first_byte, end_byte, in_use, anchor, lift, cross_kv):
    columns = anchor + jnp.arange(extended.shape[0], dtype=jnp.int32)
    inside = (
        (columns[None, :] >= first_byte[:, None])
        & (columns[None, :] < end_byte[:, None])
        & in_use[:, None]
    )
    member = inside.astype(jnp.bfloat16)
    totals = jnp.dot(member, extended, preferred_element_type=jnp.float32)
    lengths = jnp.maximum(jnp.sum(inside.astype(jnp.float32), axis=1), 1.0)
    pooled = (totals / lengths[:, None]).astype(jnp.bfloat16)
    lifted = jnp.dot(pooled, lift, preferred_element_type=jnp.float32)
    key_rows = jnp.dot(extended, cross_kv[0], preferred_element_type=jnp.float32).astype(
        jnp.bfloat16
    )
    value_rows = jnp.dot(extended, cross_kv[1], preferred_element_type=jnp.float32).astype(
        jnp.bfloat16
    )
    slot_total = first_byte.shape[0]
    head_count = lifted.shape[1] // HD
    queries = lifted.astype(jnp.bfloat16).reshape(slot_total, head_count, HD)
    scores = jnp.einsum(
        "phd,khd->hpk",
        queries,
        key_rows.reshape(-1, head_count, HD),
        preferred_element_type=jnp.float32,
    ) * (1.0 / math.sqrt(HD))
    allowed = inside | (~in_use)[:, None] & (columns[None, :] == anchor)
    weights = masked_softmax(scores, allowed[None]).astype(jnp.bfloat16)
    crossed = jnp.einsum(
        "hpk,khd->phd",
        weights,
        value_rows.reshape(-1, head_count, HD),
        preferred_element_type=jnp.float32,
    )
    crossed = crossed.reshape(slot_total, head_count * HD)
    return jnp.where(in_use[:, None], lifted + crossed, 0.0).astype(jnp.bfloat16)


def add_counts(earlier, later):
    return earlier + later


def shards(
    byte_states,
    enc_gain,
    enc_qkv,
    enc_proj_out,
    starts,
    counts,
    lift,
    cross_kv,
    latent_gain,
    lat_qkv,
    lat_proj_out,
):
    byte_rows = byte_states.shape[0]
    anchor = lax.axis_index(SEQ) * byte_rows
    states = byte_states.astype(jnp.float32)
    normed = rms_scale(states, enc_gain.astype(jnp.float32)).astype(jnp.bfloat16)
    projected = jnp.einsum(
        "bd,idc->ibc", normed, enc_qkv, preferred_element_type=jnp.float32
    ).astype(jnp.bfloat16)
    reach_blocks = max(WIN // byte_rows, 1)
    tail_rows = min(WIN, byte_rows)
    key_parts = []
    value_parts = []
    for distance in range(reach_blocks, 0, -1):
        moved_keys, moved_values = from_behind(
            (projected[1, byte_rows - tail_rows :], projected[2, byte_rows - tail_rows :]),
            SEQ,
            distance,
        )
        key_parts.append(moved_keys)
        value_parts.append(moved_values)
    key_rows = jnp.concatenate(key_parts + [projected[1]], axis=0)
    value_rows = jnp.concatenate(value_parts + [projected[2]], axis=0)
    head_count = projected.shape[2] // EH
    scores = jnp.einsum(
        "qhd,khd->hqk",
        projected[0].reshape(byte_rows, head_count, EH),
        key_rows.reshape(-1, head_count, EH),
        preferred_element_type=jnp.float32,
    ) * (1.0 / math.sqrt(EH))
    query_pos = anchor + jnp.arange(byte_rows, dtype=jnp.int32)
    key_pos = anchor - WIN + jnp.arange(WIN + byte_rows, dtype=jnp.int32)
    allowed = (
        (key_pos[None, :] <= query_pos[:, None])
        & (key_pos[None, :] > query_pos[:, None] - WIN)
        & (key_pos[None, :] >= 0)
    )
    weights = masked_softmax(scores, allowed[None]).astype(jnp.bfloat16)
    attended = jnp.einsum(
        "hqk,khd->qhd",
        weights,
        value_rows.reshape(-1, head_count, EH),
        preferred_element_type=jnp.float32,
    )
    attended = attended.reshape(byte_rows, head_count * EH).astype(jnp.bfloat16)
    blended = taken_together(
        jnp.dot(attended, enc_proj_out, preferred_element_type=jnp.float32), "tp"
    )
    encoded = (states + blended).astype(jnp.bfloat16)
    patch_count = counts[0]
    local_starts = starts[0]
    first_local = (local_starts[0:1] - anchor).astype(jnp.bfloat16)
    next_rows, next_first = from_behind((encoded[:SPILL], first_local), SEQ, -1)
    next_first = next_first.astype(jnp.int32)[0]
    extended = jnp.concatenate([encoded, next_rows], axis=0)
    slot_ids = jnp.arange(local_starts.shape[0], dtype=jnp.int32)
    in_use = slot_ids < patch_count
    following = jnp.concatenate([local_starts[1:], jnp.zeros((1,), jnp.int32)])
    patch_end = jnp.where(slot_ids + 1 < patch_count, following, anchor + byte_rows + next_first)
    patches = patch_block(extended, local_starts, patch_end, in_use, anchor, lift, cross_kv)
    offset = carried_in(counts, SEQ, add_counts, jnp.zeros((1,), jnp.int32))[0]
    position = offset + slot_ids
    slot_total = patches.shape[0]
    full_rows = gather_directly(patches, "tp", 1)
    normed_rows = rms_scale(full_rows.astype(jnp.float32), latent_gain.astype(jnp.float32)).astype(
        jnp.bfloat16
    )
    inner_width = lat_qkv.shape[2]
    projected = jnp.einsum(
        "pd,idc->ipc",
        normed_rows,
        spread_gather(lat_qkv, SEQ, 1),
        preferred_element_type=jnp.float32,
    )
    heads_here = inner_width // HD
    queries = rotate(projected[0].reshape(slot_total, heads_here, HD), position).astype(
        jnp.bfloat16
    )
    latent_keys = (
        rotate(projected[1].reshape(slot_total, heads_here, HD), position)
        .astype(jnp.bfloat16)
        .reshape(slot_total, inner_width)
    )
    latent_values = projected[2].astype(jnp.bfloat16)
    latent_pos = jnp.where(in_use, position, far_position)
    largest = jnp.full((heads_here, slot_total), -1e30, jnp.float32)
    piece_keys, piece_values, piece_pos = (
        *sent_together((latent_keys, latent_values), SEQ, 0, 1),
        lax.all_gather(shortened(latent_pos), SEQ, axis=0, tiled=True).astype(latent_pos.dtype),
    )
    rows_here = piece_keys.shape[0]
    piece_scores = jnp.einsum(
        "qhd,khd->hqk",
        queries,
        piece_keys.reshape(rows_here, heads_here, HD),
        preferred_element_type=jnp.float32,
    ) * (1.0 / math.sqrt(HD))
    permitted = (piece_pos[None, :] <= position[:, None])[None]
    piece_scores = jnp.where(permitted, piece_scores, -1e30)
    renewed = jnp.maximum(largest, jnp.max(piece_scores, axis=-1))
    raised = jnp.where(permitted, jnp.exp(piece_scores - renewed[..., None]), 0.0)
    weight_sum = jnp.sum(raised, axis=-1)
    weighted = jnp.einsum(
        "hqk,khd->hqd",
        raised.astype(jnp.bfloat16),
        piece_values.reshape(rows_here, heads_here, HD),
        preferred_element_type=jnp.float32,
    )
    largest, weight_sum, weighted = (renewed, weight_sum, weighted)
    latent_heads = (
        (weighted / weight_sum[..., None])
        .transpose(1, 0, 2)
        .reshape(slot_total, inner_width)
        .astype(jnp.bfloat16)
    )
    partials = jnp.dot(
        latent_heads,
        lax.all_gather(lat_proj_out, SEQ, axis=1, tiled=True),
        preferred_element_type=jnp.float32,
    )
    reduced = sum_at_owner(partials, "tp", 1)
    latent = jnp.where(in_use[:, None], patches.astype(jnp.float32) + reduced, 0.0).astype(
        jnp.bfloat16
    )
    return (encoded, latent)


def solution(mesh):
    finer = Mesh(mesh.devices.reshape(4, 4, 4, mesh.shape["tp"]), ("seq_0", "seq_1", "seq_2", "tp"))
    in_specs = (
        P(SEQ, None),
        P(),
        P(None, None, "tp"),
        P("tp", None),
        P(SEQ, None),
        P(SEQ),
        P(None, "tp"),
        P(None, None, "tp"),
        P(),
        P(None, SEQ, "tp"),
        P("tp", SEQ),
    )
    out_specs = (P(SEQ, None), P(SEQ, "tp"))
    return jax.shard_map(
        shards, mesh=finer, in_specs=in_specs, out_specs=out_specs, check_vma=False
    )
```

profile of v0, /device:TPU:1, one launch (start us, length us, event | category | flops | bytes accessed | tf_op | source)
XLA Modules:
  0.0 1065.7 jit_solution(14300211120696718170)
XLA Ops:
  8.3 11.9 %all-gather.3 = bf16[12,24,512]{2,1,0:T(8,128)(2,1)} all-gather(bf16[3,24,512]{2,1,0:T(8,128)(2,1)S(1)} %get-tuple-element.15), channel_id=5, replica_groups=mesh['seq_0'=4,'seq_1'=4,'seq_2'=4,'tp'=4] {'seq_1'}, dimensions={0}, use_global_device_ids=true | all-gather | bytes 368640 | tf_op jit(solution)/shard_map/all_gather | solution.py:73
  20.4 10.7 %all-gather.6 = bf16[12,24,512]{2,1,0:T(8,128)(2,1)} all-gather(bf16[3,24,512]{2,1,0:T(8,128)(2,1)S(1)} %get-tuple-element.16), channel_id=8, replica_groups=mesh['seq_0'=4,'seq_1'=4,'seq_2'=4,'tp'=4] {'seq_2'}, dimensions={0}, use_global_device_ids=true | all-gather | bytes 368640 | tf_op jit(solution)/shard_map/all_gather | solution.py:73
  31.9 13.9 %all-gather = bf16[12,16,512]{2,1,0:T(8,128)(2,1)S(1)} all-gather(bf16[3,16,512]{2,1,0:T(8,128)(2,1)S(1)} %split.15), channel_id=2, replica_groups=mesh['seq_0'=4,'seq_1'=4,'seq_2'=4,'tp'=4] {'seq_0'}, dimensions={0}, use_global_device_ids=true | all-gather | bytes 245760 | tf_op jit(solution)/shard_map/all_gather | solution.py:73
  45.8 12.3 %all-gather.1 = bf16[16,3,16,512]{3,2,1,0:T(8,128)(2,1)} all-gather(bf16[4,3,16,512]{3,2,1,0:T(8,128)(2,1)S(1)} %bitcast.170), channel_id=3, replica_groups=mesh['seq_0'=4,'seq_1'=4,'seq_2'=4,'tp'=4] {'seq_2'}, dimensions={0}, use_global_device_ids=true | all-gather | bytes 983040 | tf_op jit(solution)/shard_map/all_gather | solution.py:73
  58.2 5.4 all-gather.23.cloned.1.call-done
  66.1 3.5 collective-permute-start.2
  69.6 3.2 collective-permute-start.3
  72.8 4.2 collective-permute-start
  86.2 13.0 %all-to-all-start = ((f32[4,256,1024]{2,1,0:T(8,128)}), f32[4,256,1024]{2,1,0:T(8,128)}, u32[]{:S(2)}, u32[]{:S(2)}) async-start(f32[4,256,1024]{2,1,0:T(8,128)} %broadcast_in_dim.134), calls=%async_computation | async-start | bytes 8388608 | tf_op jit(solution)/shard_map/all_to_all | solution.py:26
  105.6 45.2 %all-to-all-done = f32[4,256,1024]{2,1,0:T(8,128)} async-done(((f32[4,256,1024]{2,1,0:T(8,128)}), f32[4,256,1024]{2,1,0:T(8,128)}, u32[]{:S(2)}, u32[]{:S(2)}) %all-to-all-start) | async-done | bytes 4194336 | tf_op jit(solution)/shard_map/all_to_all | solution.py:26
  151.4 59.0 %all-to-all-start.1 = ((s32[64,1,1]{2,1,0:T(1,128)}), s32[64,1,1]{2,1,0:T(1,128)S(1)}, u32[]{:S(2)}, u32[]{:S(2)}) async-start(s32[64,1,1]{2,1,0:T(1,128)} %broadcast_in_dim.141), calls=%async_computation.1 | async-start | bytes 65536 | tf_op jit(solution)/shard_map/all_to_all | solution.py:26
  210.4 3.2 reduce_sum.74
  216.1 3.6 collective-permute-done.5
  229.9 5.0 all-to-all-start.2
  239.3 4.0 copy.113
  243.2 11.5 %all-to-all-done.2 = bf16[4,64,1024]{2,1,0:T(8,128)(2,1)S(1)} async-done(((bf16[4,64,1024]{2,1,0:T(8,128)(2,1)}), bf16[4,64,1024]{2,1,0:T(8,128)(2,1)S(1)}, u32[]{:S(2)}, u32[]{:S(2)}) %all-to-all-start.2) | async-done | bytes 524320 | tf_op jit(solution)/shard_map/all_to_all | solution.py:26
  256.0 5.2 copy.114
  261.2 41.7 %all-gather.29.cloned.1.call-done = bf16[16,4,3,24,512]{4,3,2,1,0:T(8,128)(2,1)} async-done(((bf16[4,4,3,24,512]{4,3,2,1,0:T(8,128)(2,1)}), bf16[16,4,3,24,512]{4,3,2,1,0:T(8,128)(2,1)}) %all-gather.29.cloned.1.call-update) | async-done | bytes 4718608 | tf_op jit(solution)/shard_map/all_gather | solution.py:73
  302.9 6.3 maximum_bitcast_fusion
  316.8 316.5 %all-reduce = s32[4096]{0:T(1024)S(1)} all-reduce(s32[4096]{0:T(1024)S(1)} %select_dynamic-update-slice_fusion), channel_id=1, replica_groups=mesh['seq_0'=4,'seq_1'=4,'seq_2'=4,'tp'=4] {'seq_0','seq_1','seq_2'}, use_global_device_ids=true, to_apply=%add | all-reduce | flops 4096 | bytes 32768
  636.1 4.2 slice_bitcast_fusion.1
  644.4 343.3 %all-gather.19.cloned.1.call-done = bf16[512,4096]{0,1:T(8,128)(2,1)} async-done(((bf16[512,64]{0,1:T(8,128)(2,1)}), bf16[512,4096]{0,1:T(8,128)(2,1)}) %all-gather.19.cloned.1.call-update) | async-done | bytes 4194320 | tf_op jit(solution)/shard_map/all_gather | solution.py:320
  987.7 3.7 convolution_bitcast_fusion
  991.4 66.6 %all_to_all.24 = f32[4,64,1024]{2,1,0:T(8,128)S(1)} all-to-all(f32[4,64,1024]{2,1,0:T(8,128)S(1)} %convolution_bitcast_fusion), channel_id=1, replica_groups=mesh['seq_0'=4,'seq_1'=4,'seq_2'=4,'tp'=4] {'tp'}, dimensions={0} | all-to-all | bytes 2097152 | tf_op jit(solution)/shard_map/all_to_all | solution.py:114
  (133 shorter events, 50.8 us)
Async XLA Ops:
  7.2 215.7 %copy-start = (bf16[1024,1024]{1,0:T(8,128)(2,1)S(1)}, bf16[1024,1024]{1,0:T(8,128)(2,1)}, u32[]{:S(2)}) copy-start(bf16[1024,1024]{1,0:T(8,128)(2,1)} %param.17) | copy-start | bytes 6291460
  7.2 56.5 %copy-start.8 = (bf16[1024]{0:T(1024)(128)(2,1)S(1)}, bf16[1024]{0:T(1024)(128)(2,1)}, u32[]{:S(2)}) copy-start(bf16[1024]{0:T(1024)(128)(2,1)} %param.12) | copy-start | bytes 6148
  7.2 56.5 %copy-start.2 = (bf16[256,1024]{1,0:T(8,128)(2,1)S(1)}, bf16[256,1024]{1,0:T(8,128)(2,1)}, u32[]{:S(2)}) copy-start(bf16[256,1024]{1,0:T(8,128)(2,1)} %param.11) | copy-start | bytes 1572868
  7.2 56.4 %all-gather.23.cloned.1.call-start = ((), (), s32[]{:S(2)}) async-start(), calls=%async_computation.7 | async-start | bytes 1474560 | tf_op jit(solution)/shard_map/all_gather | solution.py:73
  20.3 78.8 %all-gather.27.cloned.1.call-start = ((), (), s32[]{:S(2)}) async-start(), calls=%async_computation.9 | async-start | bytes 1474560 | tf_op jit(solution)/shard_map/all_gather | solution.py:73
  31.1 208.2 %all-gather.21.cloned.1.call-start = ((), (), s32[]{:S(2)}) async-start(), calls=%async_computation.6 | async-start | bytes 3932160 | tf_op jit(solution)/shard_map/all_gather | solution.py:73
  58.1 197.9 %all-gather.25.cloned.1.call-start = ((), (), s32[]{:S(2)}) async-start(), calls=%async_computation.8 | async-start | bytes 5898240 | tf_op jit(solution)/shard_map/all_gather | solution.py:73
  66.1 13.7 %collective-permute-start.2 = (bf16[256,256]{0,1:T(8,128)(2,1)S(1)}, bf16[256,256]{0,1:T(8,128)(2,1)S(1)}, u32[]{:S(2)}, u32[]{:S(2)}) collective-permute-start(bf16[256,256]{0,1:T(8,128)(2,1)S(1)} %get-tuple-element.7), channel_id=1, source_target_pairs={{0,8},{4,12},{8,16},{12,20},{16,24},{20,28},{24,32},{28,36},{32,40... | collective-permute-start | bytes 393224 | tf_op jit(solution)/shard_map/ppermute | solution.py:21
  69.6 10.3 collective-permute-start.3
  72.8 9.5 collective-permute-start
  77.0 5.3 collective-permute-start.1
  86.2 13.5 %copy-start.7 = (s32[1,64]{1,0:T(1,128)S(1)}, s32[1,64]{1,0:T(1,128)}, u32[]{:S(2)}) copy-start(s32[1,64]{1,0:T(1,128)} %param.15) | copy-start | bytes 772
  86.2 15.5 %copy-start.6 = (bf16[4096]{0:T(1024)(128)(2,1)S(1)}, bf16[4096]{0:T(1024)(128)(2,1)}, u32[]{:S(2)}) copy-start(bf16[4096]{0:T(1024)(128)(2,1)} %param.19) | copy-start | bytes 24580
  86.2 64.6 %all-to-all-start = ((f32[4,256,1024]{2,1,0:T(8,128)}), f32[4,256,1024]{2,1,0:T(8,128)}, u32[]{:S(2)}, u32[]{:S(2)}) async-start(f32[4,256,1024]{2,1,0:T(8,128)} %broadcast_in_dim.134), calls=%async_computation | async-start | bytes 8388608 | tf_op jit(solution)/shard_map/all_to_all | solution.py:26
  99.1 203.8 %all-gather.29.cloned.1.call-start = ((), (), s32[]{:S(2)}) async-start(), calls=%async_computation.10 | async-start | bytes 5898240 | tf_op jit(solution)/shard_map/all_gather | solution.py:73
  99.8 4.8 collective-permute-start.4
  151.4 77.6 %all-to-all-start.1 = ((s32[64,1,1]{2,1,0:T(1,128)}), s32[64,1,1]{2,1,0:T(1,128)S(1)}, u32[]{:S(2)}, u32[]{:S(2)}) async-start(s32[64,1,1]{2,1,0:T(1,128)} %broadcast_in_dim.141), calls=%async_computation.1 | async-start | bytes 65536 | tf_op jit(solution)/shard_map/all_to_all | solution.py:26
  214.8 4.9 copy-start.3
  214.8 4.9 collective-permute-start.5
  229.9 24.8 %all-to-all-start.2 = ((bf16[4,64,1024]{2,1,0:T(8,128)(2,1)}), bf16[4,64,1024]{2,1,0:T(8,128)(2,1)S(1)}, u32[]{:S(2)}, u32[]{:S(2)}) async-start(bf16[4,64,1024]{2,1,0:T(8,128)(2,1)} %broadcast_in_dim.145), calls=%async_computation.2 | async-start | bytes 1048576 | tf_op jit(solution)/shard_map/all_to_all | solution.py:26
  234.9 401.2 %all-gather.17.cloned.1.call-start = ((), (), s32[]{:S(2)}) async-start(), calls=%async_computation.4 | async-start | bytes 8519680 | tf_op jit(solution)/shard_map/all_gather | solution.py:96
  311.0 4.3 copy-start.9
  314.5 673.1 %all-gather.19.cloned.1.call-start = ((), (), s32[]{:S(2)}) async-start(), calls=%async_computation.5 | async-start | bytes 4259840 | tf_op jit(solution)/shard_map/all_gather | solution.py:320
  987.7 71.2 %copy-start.1 = (bf16[1024,1024]{1,0:T(8,128)(2,1)S(1)}, bf16[1024,1024]{1,0:T(8,128)(2,1)}, u32[]{:S(2)}) copy-start(bf16[1024,1024]{1,0:T(8,128)(2,1)} %param.17) | copy-start | bytes 6291460
  (2 other events, 4.5 us)
Sparse Core Ops, SparseCore 0:
  20.4 43.1 all-gather.22
  65.4 24.5 all-gather.26
  91.8 47.5 all-gather.20
  141.1 55.4 all-gather.24
  198.2 104.6 all-gather.28
  314.7 321.3 all-gather.16
  637.9 349.7 all-gather.18
where the time goes:
time: 1070 us
  waiting for transfers between devices  457 us (43%)
  blocking collectives  432 us (40%)
  starting transfers between devices  93.1 us (9%)
  local copies, waits for them, and re-layouts  25.2 us (2%)
  matrix products  22 us (2%)
  other arithmetic  18.3 us (2%)
  between operations  17.9 us (2%)
    all_gather x1, waiting for transfers between devices, shards(): lax.all_gather(lat_proj_out, SEQ, axis=1, tiled=True)  343 us
    unnamed x1, blocking collectives  317 us
    all_to_all x3, starting transfers between devices, from_everyone(): return lax.all_to_all(copies, axis, split_axis=0, concat_axis=0, tiled=True)  76.9 us
    all_to_all x1, blocking collectives, sum_at_owner(): lax.all_to_all(in_blocks(value, dim, length), axis, 0, 0, tiled=True)  66.6 us
    all_to_all x3, waiting for transfers between devices, from_everyone(): return lax.all_to_all(copies, axis, split_axis=0, concat_axis=0, tiled=True)  56.7 us
    all_gather x4, blocking collectives, gather_in_order(): tiles = lax.all_gather(tiles, axes[k])  48.8 us
    all_gather x5, waiting for transfers between devices, gather_in_order(): tiles = lax.all_gather(tiles, axes[k])  47.2 us
  transfers between devices with their start and end apart: 16, of which 8 were waited for; matrix products, arithmetic and copies ran while one was open for 5% of the time, Pallas kernels for 0%

commit v1 on v0

--- a/solution.py
+++ b/solution.py
@@ -317,7 +317,9 @@
     )
     partials = jnp.dot(
         latent_heads,
-        lax.all_gather(lat_proj_out, SEQ, axis=1, tiled=True),
+        jnp.concatenate(
+            lax.all_to_all(jnp.stack([lat_proj_out] * lax.axis_size(SEQ)), SEQ, 0, 0), axis=1
+        ),
         preferred_element_type=jnp.float32,
     )
     reduced = sum_at_owner(partials, "tp", 1)

time: 1070 us -> 812 us (0.76)
  waiting for transfers between devices: 457 us -> 111 us
  blocking collectives: 432 us -> 512 us
    all_gather x1 -> x0, waiting for transfers between devices: 343 us -> none  [shards(): lax.all_gather(lat_proj_out, SEQ, axis=1, tiled=True)]
    unnamed x1, blocking collectives: 317 us -> 392 us
  transfers between devices with their start and end apart: 16 -> 16, of which waited for: 8 -> 6; matrix products, arithmetic and copies ran while one was open for 5% -> 6% of each run, Pallas kernels for 0% -> 0%
where the time goes in v1:
time: 812 us; the launch traced here: 811 us
  blocking collectives  512 us (63%)
  waiting for transfers between devices  111 us (14%)
  starting transfers between devices  102 us (13%)
  local copies, waits for them, and re-layouts  27.6 us (3%)
  matrix products  22 us (3%)
  other arithmetic  18.3 us (2%)
  between operations  17.9 us (2%)
    unnamed x1, blocking collectives  392 us
    all_to_all x3, starting transfers between devices, from_everyone(): return lax.all_to_all(copies, axis, split_axis=0, concat_axis=0, tiled=True)  76.9 us
    all_to_all x1, blocking collectives, sum_at_owner(): lax.all_to_all(in_blocks(value, dim, length), axis, 0, 0, tiled=True)  71.3 us
    all_to_all x3, waiting for transfers between devices, from_everyone(): return lax.all_to_all(copies, axis, split_axis=0, concat_axis=0, tiled=True)  56.7 us
    all_gather x4, blocking collectives, gather_in_order(): tiles = lax.all_gather(tiles, axes[k])  48.8 us
    all_gather x5, waiting for transfers between devices, gather_in_order(): tiles = lax.all_gather(tiles, axes[k])  47.2 us
  transfers between devices with their start and end apart: 16, of which 6 were waited for; matrix products, arithmetic and copies ran while one was open for 6% of the time, Pallas kernels for 0%

profile of v1, /device:TPU:1, one launch (start us, length us, event | category | flops | bytes accessed | tf_op | source)
XLA Modules:
  0.0 810.9 jit_solution(15502911659330395364)
XLA Ops:
  8.3 11.9 %all-gather.3 = bf16[12,24,512]{2,1,0:T(8,128)(2,1)} all-gather(bf16[3,24,512]{2,1,0:T(8,128)(2,1)S(1)} %get-tuple-element.15), channel_id=5, replica_groups=mesh['seq_0'=4,'seq_1'=4,'seq_2'=4,'tp'=4] {'seq_1'}, dimensions={0}, use_global_device_ids=true | all-gather | bytes 368640 | tf_op jit(solution)/shard_map/all_gather | solution.py:73
  20.4 10.7 %all-gather.6 = bf16[12,24,512]{2,1,0:T(8,128)(2,1)} all-gather(bf16[3,24,512]{2,1,0:T(8,128)(2,1)S(1)} %get-tuple-element.16), channel_id=8, replica_groups=mesh['seq_0'=4,'seq_1'=4,'seq_2'=4,'tp'=4] {'seq_2'}, dimensions={0}, use_global_device_ids=true | all-gather | bytes 368640 | tf_op jit(solution)/shard_map/all_gather | solution.py:73
  31.9 13.9 %all-gather = bf16[12,16,512]{2,1,0:T(8,128)(2,1)S(1)} all-gather(bf16[3,16,512]{2,1,0:T(8,128)(2,1)S(1)} %split.15), channel_id=2, replica_groups=mesh['seq_0'=4,'seq_1'=4,'seq_2'=4,'tp'=4] {'seq_0'}, dimensions={0}, use_global_device_ids=true | all-gather | bytes 245760 | tf_op jit(solution)/shard_map/all_gather | solution.py:73
  45.8 12.3 %all-gather.1 = bf16[16,3,16,512]{3,2,1,0:T(8,128)(2,1)} all-gather(bf16[4,3,16,512]{3,2,1,0:T(8,128)(2,1)S(1)} %bitcast.173), channel_id=3, replica_groups=mesh['seq_0'=4,'seq_1'=4,'seq_2'=4,'tp'=4] {'seq_2'}, dimensions={0}, use_global_device_ids=true | all-gather | bytes 983040 | tf_op jit(solution)/shard_map/all_gather | solution.py:73
  58.2 5.4 all-gather.20.cloned.1.call-done
  66.1 3.5 collective-permute-start.2
  69.6 3.2 collective-permute-start.3
  72.8 4.2 collective-permute-start
  86.2 13.0 %all-to-all-start = ((f32[4,256,1024]{2,1,0:T(8,128)}), f32[4,256,1024]{2,1,0:T(8,128)}, u32[]{:S(2)}, u32[]{:S(2)}) async-start(f32[4,256,1024]{2,1,0:T(8,128)} %broadcast_in_dim.134), calls=%async_computation | async-start | bytes 8388608 | tf_op jit(solution)/shard_map/all_to_all | solution.py:26
  105.6 45.2 %all-to-all-done = f32[4,256,1024]{2,1,0:T(8,128)} async-done(((f32[4,256,1024]{2,1,0:T(8,128)}), f32[4,256,1024]{2,1,0:T(8,128)}, u32[]{:S(2)}, u32[]{:S(2)}) %all-to-all-start) | async-done | bytes 4194336 | tf_op jit(solution)/shard_map/all_to_all | solution.py:26
  151.4 59.0 %all-to-all-start.1 = ((s32[64,1,1]{2,1,0:T(1,128)}), s32[64,1,1]{2,1,0:T(1,128)S(1)}, u32[]{:S(2)}, u32[]{:S(2)}) async-start(s32[64,1,1]{2,1,0:T(1,128)} %broadcast_in_dim.141), calls=%async_computation.1 | async-start | bytes 65536 | tf_op jit(solution)/shard_map/all_to_all | solution.py:26
  210.4 3.2 reduce_sum.74
  216.1 3.6 collective-permute-done.5
  229.9 5.0 all-to-all-start.2
  239.3 4.0 copy.113
  243.2 11.5 %all-to-all-done.2 = bf16[4,64,1024]{2,1,0:T(8,128)(2,1)S(1)} async-done(((bf16[4,64,1024]{2,1,0:T(8,128)(2,1)}), bf16[4,64,1024]{2,1,0:T(8,128)(2,1)S(1)}, u32[]{:S(2)}, u32[]{:S(2)}) %all-to-all-start.2) | async-done | bytes 524320 | tf_op jit(solution)/shard_map/all_to_all | solution.py:26
  256.0 5.2 copy.114
  261.2 41.7 %all-gather.26.cloned.1.call-done = bf16[16,4,3,24,512]{4,3,2,1,0:T(8,128)(2,1)} async-done(((bf16[4,4,3,24,512]{4,3,2,1,0:T(8,128)(2,1)}), bf16[16,4,3,24,512]{4,3,2,1,0:T(8,128)(2,1)}) %all-gather.26.cloned.1.call-update) | async-done | bytes 4718608 | tf_op jit(solution)/shard_map/all_gather | solution.py:73
  302.9 6.3 maximum_bitcast_fusion
  317.0 9.1 %all-to-all-start.3 = ((bf16[64,512,64]{1,2,0:T(8,128)(2,1)}), bf16[64,512,64]{1,2,0:T(8,128)(2,1)}, u32[]{:S(2)}, u32[]{:S(2)}) async-start(bf16[64,512,64]{1,2,0:T(8,128)(2,1)} %stack.2), calls=%async_computation.3 | async-start | bytes 8388608 | tf_op jit(solution)/shard_map/all_to_all | solution.py:321
  327.6 392.1 %all-reduce = s32[4096]{0:T(1024)S(1)} all-reduce(s32[4096]{0:T(1024)S(1)} %select_dynamic-update-slice_fusion), channel_id=1, replica_groups=mesh['seq_0'=4,'seq_1'=4,'seq_2'=4,'tp'=4] {'seq_0','seq_1','seq_2'}, use_global_device_ids=true, to_apply=%add | all-reduce | flops 4096 | bytes 32768
  719.9 4.2 slice_bitcast_fusion.1
  728.3 3.7 convolution_bitcast_fusion
  732.0 71.3 %all_to_all.29 = f32[4,64,1024]{2,1,0:T(8,128)S(1)} all-to-all(f32[4,64,1024]{2,1,0:T(8,128)S(1)} %convolution_bitcast_fusion), channel_id=1, replica_groups=mesh['seq_0'=4,'seq_1'=4,'seq_2'=4,'tp'=4] {'tp'}, dimensions={0} | all-to-all | bytes 2097152 | tf_op jit(solution)/shard_map/all_to_all | solution.py:114
  (135 shorter events, 50.1 us)
Async XLA Ops:
  7.2 215.7 %copy-start = (bf16[1024,1024]{1,0:T(8,128)(2,1)S(1)}, bf16[1024,1024]{1,0:T(8,128)(2,1)}, u32[]{:S(2)}) copy-start(bf16[1024,1024]{1,0:T(8,128)(2,1)} %param.17) | copy-start | bytes 6291460
  7.2 56.5 %copy-start.9 = (bf16[1024]{0:T(1024)(128)(2,1)S(1)}, bf16[1024]{0:T(1024)(128)(2,1)}, u32[]{:S(2)}) copy-start(bf16[1024]{0:T(1024)(128)(2,1)} %param.12) | copy-start | bytes 6148
  7.2 56.5 %copy-start.2 = (bf16[256,1024]{1,0:T(8,128)(2,1)S(1)}, bf16[256,1024]{1,0:T(8,128)(2,1)}, u32[]{:S(2)}) copy-start(bf16[256,1024]{1,0:T(8,128)(2,1)} %param.11) | copy-start | bytes 1572868
  7.2 56.4 %all-gather.20.cloned.1.call-start = ((), (), s32[]{:S(2)}) async-start(), calls=%async_computation.7 | async-start | bytes 1474560 | tf_op jit(solution)/shard_map/all_gather | solution.py:73
  20.3 78.8 %all-gather.24.cloned.1.call-start = ((), (), s32[]{:S(2)}) async-start(), calls=%async_computation.9 | async-start | bytes 1474560 | tf_op jit(solution)/shard_map/all_gather | solution.py:73
  31.1 208.2 %all-gather.18.cloned.1.call-start = ((), (), s32[]{:S(2)}) async-start(), calls=%async_computation.6 | async-start | bytes 3932160 | tf_op jit(solution)/shard_map/all_gather | solution.py:73
  58.1 197.9 %all-gather.22.cloned.1.call-start = ((), (), s32[]{:S(2)}) async-start(), calls=%async_computation.8 | async-start | bytes 5898240 | tf_op jit(solution)/shard_map/all_gather | solution.py:73
  66.1 13.7 %collective-permute-start.2 = (bf16[256,256]{0,1:T(8,128)(2,1)S(1)}, bf16[256,256]{0,1:T(8,128)(2,1)S(1)}, u32[]{:S(2)}, u32[]{:S(2)}) collective-permute-start(bf16[256,256]{0,1:T(8,128)(2,1)S(1)} %get-tuple-element.7), channel_id=1, source_target_pairs={{0,8},{4,12},{8,16},{12,20},{16,24},{20,28},{24,32},{28,36},{32,40... | collective-permute-start | bytes 393224 | tf_op jit(solution)/shard_map/ppermute | solution.py:21
  69.6 10.3 %collective-permute-start.3 = (bf16[256,256]{0,1:T(8,128)(2,1)S(1)}, bf16[256,256]{0,1:T(8,128)(2,1)S(1)}, u32[]{:S(2)}, u32[]{:S(2)}) collective-permute-start(bf16[256,256]{0,1:T(8,128)(2,1)S(1)} %get-tuple-element.7), channel_id=1, source_target_pairs={{0,4},{4,8},{8,12},{12,16},{16,20},{20,24},{24,28},{28,32},{32,36}... | collective-permute-start | bytes 393224 | tf_op jit(solution)/shard_map/ppermute | solution.py:21
  72.8 9.5 %collective-permute-start = (bf16[256,256]{0,1:T(8,128)(2,1)S(1)}, bf16[256,256]{0,1:T(8,128)(2,1)S(1)}, u32[]{:S(2)}, u32[]{:S(2)}) collective-permute-start(bf16[256,256]{0,1:T(8,128)(2,1)S(1)} %get-tuple-element.6), channel_id=1, source_target_pairs={{0,8},{4,12},{8,16},{12,20},{16,24},{20,28},{24,32},{28,36},{32,40... | collective-permute-start | bytes 393224 | tf_op jit(solution)/shard_map/ppermute | solution.py:21
  77.0 5.3 collective-permute-start.1
  86.2 13.5 %copy-start.8 = (s32[1,64]{1,0:T(1,128)S(1)}, s32[1,64]{1,0:T(1,128)}, u32[]{:S(2)}) copy-start(s32[1,64]{1,0:T(1,128)} %param.15) | copy-start | bytes 772
  86.2 15.5 %copy-start.7 = (bf16[4096]{0:T(1024)(128)(2,1)S(1)}, bf16[4096]{0:T(1024)(128)(2,1)}, u32[]{:S(2)}) copy-start(bf16[4096]{0:T(1024)(128)(2,1)} %param.19) | copy-start | bytes 24580
  86.2 64.6 %all-to-all-start = ((f32[4,256,1024]{2,1,0:T(8,128)}), f32[4,256,1024]{2,1,0:T(8,128)}, u32[]{:S(2)}, u32[]{:S(2)}) async-start(f32[4,256,1024]{2,1,0:T(8,128)} %broadcast_in_dim.134), calls=%async_computation | async-start | bytes 8388608 | tf_op jit(solution)/shard_map/all_to_all | solution.py:26
  99.1 203.8 %all-gather.26.cloned.1.call-start = ((), (), s32[]{:S(2)}) async-start(), calls=%async_computation.10 | async-start | bytes 5898240 | tf_op jit(solution)/shard_map/all_gather | solution.py:73
  99.8 4.8 collective-permute-start.4
  151.4 77.6 %all-to-all-start.1 = ((s32[64,1,1]{2,1,0:T(1,128)}), s32[64,1,1]{2,1,0:T(1,128)S(1)}, u32[]{:S(2)}, u32[]{:S(2)}) async-start(s32[64,1,1]{2,1,0:T(1,128)} %broadcast_in_dim.141), calls=%async_computation.1 | async-start | bytes 65536 | tf_op jit(solution)/shard_map/all_to_all | solution.py:26
  214.8 4.9 copy-start.3
  214.8 4.9 collective-permute-start.5
  229.9 24.8 %all-to-all-start.2 = ((bf16[4,64,1024]{2,1,0:T(8,128)(2,1)}), bf16[4,64,1024]{2,1,0:T(8,128)(2,1)S(1)}, u32[]{:S(2)}, u32[]{:S(2)}) async-start(bf16[4,64,1024]{2,1,0:T(8,128)(2,1)} %broadcast_in_dim.145), calls=%async_computation.2 | async-start | bytes 1048576 | tf_op jit(solution)/shard_map/all_to_all | solution.py:26
  234.9 485.0 %all-gather.16.cloned.1.call-start = ((), (), s32[]{:S(2)}) async-start(), calls=%async_computation.5 | async-start | bytes 8519680 | tf_op jit(solution)/shard_map/all_gather | solution.py:96
  317.0 9.1 %copy-start.10 = (u32[256]{0:T(256)S(1)}, u32[256]{0:T(256)}, u32[]{:S(2)}) copy-start(u32[256]{0:T(256)} %constant.69) | copy-start | bytes 3076
  317.0 411.2 %all-to-all-start.3 = ((bf16[64,512,64]{1,2,0:T(8,128)(2,1)}), bf16[64,512,64]{1,2,0:T(8,128)(2,1)}, u32[]{:S(2)}, u32[]{:S(2)}) async-start(bf16[64,512,64]{1,2,0:T(8,128)(2,1)} %stack.2), calls=%async_computation.3 | async-start | bytes 8388608 | tf_op jit(solution)/shard_map/all_to_all | solution.py:321
  728.2 75.8 %copy-start.1 = (bf16[1024,1024]{1,0:T(8,128)(2,1)S(1)}, bf16[1024,1024]{1,0:T(8,128)(2,1)}, u32[]{:S(2)}) copy-start(bf16[1024,1024]{1,0:T(8,128)(2,1)} %param.17) | copy-start | bytes 6291460
  (3 other events, 8.0 us)
Sparse Core Ops, SparseCore 0:
  20.4 43.1 all-gather.19
  65.4 24.5 all-gather.23
  91.8 47.5 all-gather.17
  141.1 55.4 all-gather.21
  198.2 104.6 all-gather.25
  314.7 360.1 all-gather.15
